TPU v7x, 32 devices: a whole 2x2x4 slice. The times are simulated.
32 devices in a mesh: grp: 1, date: 4 (over y, x), shard: 8 (over z, core).
Axes of the slice: x: 2, y: 2, z: 4, core: 2. Of those that a mesh axis runs over, the one named last changes fastest.
Arguments:
- echo_spectra: bfloat16 [4, 2, 128, 8192], P(('grp', 'date'), None, 'shard'), may hold values from -6 to 6
- range_reference: float32 [2, 8192], replicated, may hold values from -5 to 5
- azimuth_reference: bfloat16 [2, 128, 8192], P(None, None, 'shard'), may hold values from -5 to 5
- block_owner: int32 [4, 64], P(('grp', 'date')), may hold values from 0 to 7, as said below
- block_slot: int32 [4, 64], P(('grp', 'date')), may hold values from 0 to 15, as said below
- kernel_index: int32 [4, 64], P(('grp', 'date')), may hold values from 0 to 7
Outputs:
- filtered: bfloat16 [4, 128, 2, 2, 128, 128], P(('grp', 'date'), 'shard')
Inputs may be any that keep to these rules, and one draw needn't show every extreme that they name: `block_owner`: every date carries the same owners (the stack is coregistered onto one map grid). Within a date, the 8 blocks of one range-column group name any one owner at most 2 times, and some group names some owner exactly 2 times; every owner is named by at most 16 blocks, and some owner by exactly 16. `block_slot`: every date carries the same slots. Within a date, blocks that name the same owner have distinct slots.
All inputs are finite; a program needn't handle non-finite values.
Results may differ from a plain program's by a relative error of at most 0.017.
Values may be sent and summed in bfloat16 or wider, within the bound.
A program may use at most 128 MiB of HBM per device.

v0:
```python
import functools
import math

import jax
import jax.numpy as jnp
import ml_dtypes
import numpy as np
from jax import lax
from jax.experimental import pallas as pl
from jax.experimental.pallas import tpu as pltpu
from jax.sharding import PartitionSpec as P

BLK = 128
NSUB = 8
BLK_DEV = 8
BF = jnp.bfloat16
F32 = jnp.float32


def dft_parts(size, sign):
    index = np.arange(size)
    angle = 2.0 * math.pi / size * (index[:, None] * index[None, :] % size)
    scale = 1.0 / math.sqrt(size)
    return np.cos(angle) * scale, sign * np.sin(angle) * scale


def left_table(size, sign):
    cosine, sine = dft_parts(size, sign)
    return np.block([[cosine, -sine], [sine, cosine]]).astype(ml_dtypes.bfloat16)


def right_table(size, sign):
    return np.ascontiguousarray(left_table(size, sign).T)


def first_table(rng):
    outer, inner = BLK, rng // BLK
    low = outer * BLK // rng
    cosine, sine = dft_parts(outer, 1)
    full = np.stack([np.stack([cosine, sine], 1), np.stack([-sine, cosine], 1)])
    full = full.reshape(2, outer // low, low, 2 * outer)
    return np.transpose(full, (2, 0, 1, 3)).reshape(2 * outer, 2 * outer).astype(ml_dtypes.bfloat16)


def twiddle_table(rng):
    inner = rng // BLK
    phase = np.arange(inner)[:, None] * np.arange(BLK)[None, :] % rng
    angle = 2.0 * math.pi / rng * phase
    return np.stack([np.cos(angle), np.sin(angle)]).astype(np.float32)


def kernel_table():
    offset = (np.arange(NSUB) + 0.5) / NSUB
    cells = np.arange(BLK)
    dist = cells[None, None, :] - cells[None, :, None] - offset[:, None, None]
    window = np.where(np.abs(dist) < 4.0, 0.5 + 0.5 * np.cos(math.pi * dist / 4.0), 0.0)
    return (np.sinc(dist) * window).astype(ml_dtypes.bfloat16)


def flipped(a, b, n):
    total = 0
    bit = 1
    while bit < n:
        total = total + (a // bit + b // bit) % 2 * bit
        bit *= 2
    return total


def mm(left, right):
    return jnp.dot(left, right, preferred_element_type=F32)


def kernel(
    n,
    dates,
    most,
    capacity,
    owner_ref,
    slot_ref,
    kinds_ref,
    echo_ref,
    rref_ref,
    aref_ref,
    t1_ref,
    tw_ref,
    w2_ref,
    pf_ref,
    pb_ref,
    kt_ref,
    gfl_ref,
    gfr_ref,
    gbl_ref,
    gbr_ref,
    fil_hbm,
    entry_ref,
    fil,
    src_ref,
    kind_ref,
    lhs,
    mat,
    snd,
    cols,
    blocks,
    outbox,
    inbox,
    ybox,
    xbox,
    sw,
    s1,
    r1,
    s2,
    r2,
    sy,
    ry,
    sx,
    rx,
):
    me = lax.axis_index("shard")
    day = lax.axis_index("date")
    grp = lax.axis_index("grp")
    relay = dates == 4
    ydst = lax.rem(day + dates - 2, dates)
    if relay:
        parity = lax.rem(day, 2)
        xdst = day + 1 - 2 * parity
        xsrc = xdst
    else:
        xdst = lax.rem(day + dates - 1, dates)
        xsrc = lax.rem(day + 1, dates)
    ysrc = lax.rem(day + 2, dates)
    mesh_id = pl.DeviceIdType.MESH

    barrier = pltpu.get_barrier_semaphore()

    def greet(k, _):
        pl.semaphore_signal(
            barrier, inc=1, device_id=(grp, day, flipped(me, k, n)), device_id_type=mesh_id
        )
        return 0

    lax.fori_loop(1, n, greet, 0)
    for other in (ysrc, xsrc):
        pl.semaphore_signal(barrier, inc=1, device_id=(grp, other, me), device_id_type=mesh_id)

    pulses = echo_ref.shape[1]
    rng = echo_ref.shape[2]
    tiles = rng // BLK
    inner = rng // BLK
    mine = tiles // n
    wide = n * pulses

    real = echo_ref[0].astype(F32)
    imag = echo_ref[1].astype(F32)
    rre = rref_ref[0:1, :]
    rim = rref_ref[1:2, :]
    mat[0] = (real * rre + imag * rim).reshape(pulses, tiles, BLK)
    mat[1] = (imag * rre - real * rim).reshape(pulses, tiles, BLK)

    for p in range(pulses):
        both = jnp.concatenate([mat[0, p], mat[1, p]], axis=0).T
        low = BLK // inner
        parts = [both[x * inner : (x + 1) * inner] for x in range(low)]
        lhs[p * inner : (p + 1) * inner, :] = jnp.concatenate(parts, axis=1).astype(BF)

    twc = tw_ref[0]
    tws = tw_ref[1]
    group = 4
    for g in range(0, pulses, group):
        section = mm(lhs[g * inner : (g + group) * inner, :], t1_ref[...])
        rights = []
        for p in range(group):
            sre = section[p * inner : (p + 1) * inner, :BLK]
            sim = section[p * inner : (p + 1) * inner, BLK:]
            rights.append(
                jnp.concatenate([sre * twc - sim * tws, sre * tws + sim * twc], axis=0).astype(BF)
            )
        second = mm(w2_ref[...], jnp.concatenate(rights, axis=1))
        for p in range(group):
            mat[:, g + p] = second[:, p * BLK : (p + 1) * BLK].reshape(2, tiles, BLK)
    for c in range(2):
        snd[c] = jnp.swapaxes(mat[c], 0, 1).astype(BF)

    pl.semaphore_wait(barrier, n + 1)

    def copy_one(k):
        dest = flipped(me, k, n)
        return pltpu.make_async_remote_copy(
            src_ref=snd.at[:, pl.ds(dest * mine, mine)],
            dst_ref=cols.at[:, :, pl.ds(me * pulses, pulses)],
            send_sem=s1.at[k],
            recv_sem=r1.at[k],
            device_id=(grp, day, dest),
            device_id_type=mesh_id,
        )

    def wait_one(k):
        source = flipped(me, k, n)
        return pltpu.make_async_remote_copy(
            src_ref=snd.at[:, pl.ds(me * mine, mine)],
            dst_ref=cols.at[:, :, pl.ds(source * pulses, pulses)],
            send_sem=s1.at[k],
            recv_sem=r1.at[k],
            device_id=(grp, day, source),
            device_id_type=mesh_id,
        )

    def start_one(k, _):
        copy_one(k).start()
        return 0

    def end_one(k, _):
        wait_one(k).wait_recv()
        return 0

    lax.fori_loop(1, n, start_one, 0)
    cols[:, :, pl.ds(me * pulses, pulses)] = snd[:, pl.ds(me * mine, mine)]

    def sources(k, _):
        dest = flipped(me, k, n)
        seen = jnp.int32(0)
        found = [jnp.int32(0)] * most
        for b in range(BLK_DEV):
            named = owner_ref[0, me * BLK_DEV + b] == dest
            for r in range(most):
                found[r] = jnp.where(named & (seen == r), b, found[r])
            seen = seen + named.astype(jnp.int32)
        for r in range(most):
            src_ref[k * most + r] = found[r]
            kind_ref[k * most + r] = kinds_ref[0, me * BLK_DEV + found[r]]
        return 0

    lax.fori_loop(0, n, sources, 0)

    def entries(t, held):
        held = list(held)
        at = flipped(me, t, n) * most
        for b in range(BLK_DEV):
            named = owner_ref[0, t * BLK_DEV + b] == me
            slot = jnp.where(named, slot_ref[0, t * BLK_DEV + b], -1)
            for q in range(capacity):
                held[q] = jnp.where(slot == q, at, held[q])
            at = at + named.astype(jnp.int32)
        return tuple(held)

    held = lax.fori_loop(0, n, entries, (jnp.int32(n * most),) * capacity)
    for q in range(capacity):
        entry_ref[q] = held[q]
    fil[n * most] = jnp.zeros_like(fil[n * most])

    def write(e):
        return pltpu.make_async_copy(fil.at[e], fil_hbm.at[e], sw.at[e])

    write(n * most).start()
    lax.fori_loop(1, n, end_one, 0)

    rows_of = wide // BLK
    for j in range(0, mine, 2):
        right = jnp.concatenate(
            [
                jnp.concatenate([cols[0, j], cols[1, j]], axis=0),
                jnp.concatenate([cols[0, j + 1], cols[1, j + 1]], axis=0),
            ],
            axis=1,
        )
        doppler = mm(pf_ref[...], right)
        are = aref_ref[0, :, j * BLK : (j + 2) * BLK].astype(F32)
        aim = aref_ref[1, :, j * BLK : (j + 2) * BLK].astype(F32)
        dre = doppler[:wide]
        dim = doppler[wide:]
        shaped = jnp.concatenate([dre * are - dim * aim, dre * aim + dim * are], axis=0).astype(BF)
        image = mm(pb_ref[...], shaped).astype(BF)
        for x in range(2):
            for y in range(rows_of):
                for c in range(2):
                    low = c * wide + y * BLK
                    blocks[y * mine + j + x, :, c * BLK : (c + 1) * BLK] = image[
                        low : low + BLK, x * BLK : (x + 1) * BLK
                    ]

    def resampled(at):
        return mm(kt_ref[kind_ref[at]], blocks[src_ref[at]]).astype(BF)

    total = n * most
    for e in range(most):
        inbox[e] = resampled(e)

    def copy_two(e):
        return pltpu.make_async_remote_copy(
            src_ref=outbox.at[e],
            dst_ref=inbox.at[e],
            send_sem=s2.at[e],
            recv_sem=r2.at[e],
            device_id=(grp, day, flipped(me, e // most, n)),
            device_id_type=mesh_id,
        )

    def start_two(e, _):
        outbox[e] = resampled(e)
        copy_two(e).start()
        return 0

    lax.fori_loop(most, total, start_two, 0)

    def copy_y(k):
        return pltpu.make_async_remote_copy(
            src_ref=inbox.at[k],
            dst_ref=ybox.at[k],
            send_sem=sy.at[k],
            recv_sem=ry.at[k],
            device_id=(grp, ydst, me),
            device_id_type=mesh_id,
        )

    def copy_x(k, source):
        return pltpu.make_async_remote_copy(
            src_ref=source.at[k],
            dst_ref=xbox.at[k],
            send_sem=sx.at[k],
            recv_sem=rx.at[k],
            device_id=(grp, xdst, me),
            device_id_type=mesh_id,
        )

    def stage_a(k):
        if not isinstance(k, int) or k >= most:
            copy_two(k).wait_recv()
        copy_y(k).start()
        if relay:

            @pl.when(parity == 1)
            def _():
                copy_x(k, inbox).start()
        else:
            copy_x(k, inbox).start()

    def stage_b(k):
        copy_y(k).wait_recv()
        if relay:

            @pl.when(parity == 0)
            def _():
                copy_x(k, ybox).start()

    def patches(at):
        own = inbox[at].astype(F32)
        ore = own[:, :BLK]
        oim = own[:, BLK:]
        tops = []
        lows = []
        for box in (xbox, ybox):
            oth = box[at].astype(F32)
            tre = oth[:, :BLK]
            tim = oth[:, BLK:]
            tops.append(ore * tre + oim * tim)
            lows.append(oim * tre - ore * tim)
        pair = jnp.concatenate(
            [jnp.concatenate(tops, axis=1), jnp.concatenate(lows, axis=1)], axis=0
        ).astype(BF)

        def turned(x):
            return jnp.concatenate(
                [
                    jnp.concatenate([x[:BLK, :BLK], x[BLK:, :BLK]], axis=1),
                    jnp.concatenate([x[:BLK, BLK:], x[BLK:, BLK:]], axis=1),
                ],
                axis=0,
            )

        rows = mm(gfl_ref[...], pair).astype(BF)
        spectrum = mm(turned(rows), gfr_ref[...])
        weighted = []
        for x in range(2):
            spec = spectrum[x * BLK : (x + 1) * BLK]
            sre = spec[:, :BLK]
            sim = spec[:, BLK:]
            power = sre * sre + sim * sim
            line = power + pltpu.roll(power, 1, 1) + pltpu.roll(power, BLK - 1, 1)
            smooth = (line + pltpu.roll(line, 1, 0) + pltpu.roll(line, BLK - 1, 0)) * (1.0 / 9.0)
            level = jnp.sum(jnp.sum(smooth, axis=0, keepdims=True), axis=1, keepdims=True)
            level = level * (1.0 / (BLK * BLK)) + 1e-06
            weight = lax.rsqrt(lax.rsqrt(smooth * (1.0 / level)))
            weighted.append(jnp.concatenate([sre * weight, sim * weight], axis=1))
        weighted = jnp.concatenate(weighted, axis=0).astype(BF)
        back = mm(gbl_ref[...], turned(weighted)).astype(BF)
        done = mm(turned(back), gbr_ref[...]).astype(BF)
        for x in range(2):
            for c in range(2):
                fil[at, x, c] = done[x * BLK : (x + 1) * BLK, c * BLK : (c + 1) * BLK]

    def stage_c(k):
        copy_x(k, inbox).wait_recv()
        patches(k)
        write(k).start()

    def many(stage, first, stop):
        def one(k, _):
            stage(k)
            return 0

        lax.fori_loop(first, stop, one, 0)

    for e in range(most):
        stage_a(e)
    many(stage_a, most, 4)

    def opening(e, _):
        stage_a(e + 4)
        stage_b(e)
        return 0

    lax.fori_loop(0, 4, opening, 0)

    def middle(e, _):
        stage_c(e)
        stage_b(e + 4)
        return 0

    lax.fori_loop(0, 2, middle, 0)
    stage_c(2)

    def step(e, _):
        stage_a(e)
        stage_b(e - 2)
        stage_c(e - 5)
        return 0

    lax.fori_loop(8, total, step, 0)
    stage_b(total - 2)
    stage_c(total - 5)
    stage_b(total - 1)
    many(stage_c, total - 4, total)

    def drain(k, _):
        copy_y(k).wait_send()
        copy_x(k, inbox).wait_send()
        return 0

    def drain_one(k, _):
        copy_one(k).wait_send()
        return 0

    def drain_two(k, _):
        copy_two(k).wait_send()
        return 0

    lax.fori_loop(1, n, drain_one, 0)
    lax.fori_loop(most, total, drain_two, 0)
    lax.fori_loop(0, total, drain, 0)

    def written(k, _):
        write(k).wait()
        return 0

    lax.fori_loop(0, total + 1, written, 0)


def place(capacity, entry_ref, fil, out_ref, sems):
    def copy(q):
        return pltpu.make_async_copy(fil.at[entry_ref[q]], out_ref.at[q], sems.at[q])

    for q in range(capacity):
        copy(q).start()
    for q in range(capacity):
        copy(q).wait()


def body(dates, echo_spectra, range_reference, azimuth_reference, block_owner, block_slot, kernel_index):
    n = lax.axis_size("shard")
    most = max(2, 2 * BLK_DEV // n)
    capacity = min(2 * BLK_DEV, n * most)
    echo = echo_spectra[0]
    pulses, rng = echo.shape[1:]
    inner = rng // BLK
    mine = rng // BLK // n
    wide = pulses * n
    tables = [
        first_table(rng),
        twiddle_table(rng),
        left_table(inner, 1),
        left_table(wide, -1),
        left_table(wide, 1),
        kernel_table(),
        left_table(BLK, -1),
        right_table(BLK, -1),
        left_table(BLK, 1),
        right_table(BLK, 1),
    ]
    smem = pl.BlockSpec(memory_space=pltpu.SMEM)
    vmem = pl.BlockSpec(memory_space=pltpu.VMEM)
    hbm = pl.BlockSpec(memory_space=pl.ANY)
    box = pltpu.VMEM((n * most, BLK, 2 * BLK), BF)
    sems = pltpu.SemaphoreType.DMA((n,))
    tables = [jnp.asarray(t) for t in tables]
    operands = [block_owner, block_slot, kernel_index, echo, range_reference, azimuth_reference]
    operands += tables
    filtered, entry = pl.pallas_call(
        functools.partial(kernel, n, dates, most, capacity),
        out_shape=(
            jax.ShapeDtypeStruct((n * most + 1, 2, 2, BLK, BLK), BF),
            jax.ShapeDtypeStruct((capacity,), jnp.int32),
        ),
        in_specs=[smem] * 3 + [vmem] * 13,
        out_specs=(hbm, smem),
        scratch_shapes=[
            pltpu.VMEM((n * most + 1, 2, 2, BLK, BLK), BF),
            pltpu.SMEM((n * most,), jnp.int32),
            pltpu.SMEM((n * most,), jnp.int32),
            pltpu.VMEM((pulses * inner, 2 * BLK), BF),
            pltpu.VMEM((2, pulses, rng // BLK, BLK), F32),
            pltpu.VMEM((2, rng // BLK, pulses, BLK), BF),
            pltpu.VMEM((2, mine, wide, BLK), BF),
            pltpu.VMEM((BLK_DEV, BLK, 2 * BLK), BF),
            box,
            box,
            box,
            box,
            pltpu.SemaphoreType.DMA((n * most + 1,)),
            sems,
            sems,
            *[pltpu.SemaphoreType.DMA((n * most,))] * 6,
        ],
        compiler_params=pltpu.CompilerParams(collective_id=0, has_side_effects=True),
    )(
        *operands
    )
    out = pl.pallas_call(
        functools.partial(place, capacity),
        out_shape=jax.ShapeDtypeStruct((capacity, 2, 2, BLK, BLK), BF),
        in_specs=[smem, vmem],
        out_specs=pl.BlockSpec(memory_space=pl.ANY),
        scratch_shapes=[pltpu.SemaphoreType.DMA((capacity,))],
    )(entry, filtered)
    return out[None]


def solution(mesh):
    in_specs = (
        P(("grp", "date"), None, "shard", None),
        P(),
        P(None, None, "shard"),
        P(("grp", "date"), None),
        P(("grp", "date"), None),
        P(("grp", "date"), None),
    )
    out_specs = P(("grp", "date"), "shard", None, None, None, None)
    return jax.shard_map(
        functools.partial(body, mesh.shape["date"]),
        mesh=mesh,
        in_specs=in_specs,
        out_specs=out_specs,
        check_vma=False,
    )
```

profile of v0, /device:TPU:2, one launch (start us, length us, event | category | flops | bytes accessed | tf_op | source)
XLA Modules:
  0.0 58.6 jit_solution(8563641768106785581)
XLA Ops:
  0.0 55.5 %shard_map.154 = (bf16[17,2,2,128,128]{4,3,2,1,0:T(8,128)(2,1)}, s32[16]{0:T(128)}) custom-call(s32[1,64]{1,0:T(1,128)} %owner_ref.1, s32[1,64]{1,0:T(1,128)} %slot_ref.1, s32[1,64]{1,0:T(1,128)} %kinds_ref.1, bf16[2,16,8192]{2,1,0:T(8,128)(2,1)} %bitcast.2, f32[2,8192]{1,0:T(2,128)} %rref_ref.1, bf16[2,128,1024]{2,1,0:T(8,128)(2,1)} %aref_ref.1, ...), custom_call_target="tpu_custom_call" | custom-call | tf_op jit(solution)/shard_map/pallas_call | solution.py:496
  55.5 3.1 %shard_map.155 = bf16[16,2,2,128,128]{4,3,2,1,0:T(8,128)(2,1)} custom-call(s32[16]{0:T(128)} %get-tuple-element.7.entry_ref, bf16[17,2,2,128,128]{4,3,2,1,0:T(8,128)(2,1)} %get-tuple-element.8.fil), custom_call_target="tpu_custom_call" | custom-call | tf_op jit(solution)/shard_map/pallas_call | solution.py:526
where the time goes:
time: 59.7 us; the launch traced here: 58.6 us
  Pallas kernels  58.6 us (98%)
    pallas_call x1, Pallas kernels, body(): pl.pallas_call(functools.partial(kernel, n, dates, most, capacity), out_s...  55.5 us
    pallas_call x1, Pallas kernels, body(): pl.pallas_call(functools.partial(place, capacity), out_shape=jax.ShapeDty...  3.08 us

commit v1 on v0

v1 whole, which is shorter than its diff:
```python
import functools
import math

import jax
import jax.numpy as jnp
import ml_dtypes
import numpy as np
from jax import lax
from jax.experimental import pallas as pl
from jax.experimental.pallas import tpu as pltpu
from jax.sharding import PartitionSpec as P

BLK = 128
NSUB = 8
BF = jnp.bfloat16
F32 = jnp.float32


def dft_parts(size, sign):
    index = np.arange(size)
    angle = 2.0 * math.pi / size * (index[:, None] * index[None, :] % size)
    scale = 1.0 / math.sqrt(size)
    return np.cos(angle) * scale, sign * np.sin(angle) * scale


def left_table(size, sign):
    cosine, sine = dft_parts(size, sign)
    return np.block([[cosine, -sine], [sine, cosine]]).astype(ml_dtypes.bfloat16)


def right_table(size, sign):
    return np.ascontiguousarray(left_table(size, sign).T)


def first_table(rng):
    outer, inner = BLK, rng // BLK
    low = outer * BLK // rng
    cosine, sine = dft_parts(outer, 1)
    full = np.stack([np.stack([cosine, sine], 1), np.stack([-sine, cosine], 1)])
    full = full.reshape(2, outer // low, low, 2 * outer)
    return np.transpose(full, (2, 0, 1, 3)).reshape(2 * outer, 2 * outer).astype(ml_dtypes.bfloat16)


def twiddle_table(rng):
    inner = rng // BLK
    phase = np.arange(inner)[:, None] * np.arange(BLK)[None, :] % rng
    angle = 2.0 * math.pi / rng * phase
    return np.stack([np.cos(angle), np.sin(angle)]).astype(np.float32)


def kernel_table():
    offset = (np.arange(NSUB) + 0.5) / NSUB
    cells = np.arange(BLK)
    dist = cells[None, None, :] - cells[None, :, None] - offset[:, None, None]
    window = np.where(np.abs(dist) < 4.0, 0.5 + 0.5 * np.cos(math.pi * dist / 4.0), 0.0)
    return (np.sinc(dist) * window).astype(ml_dtypes.bfloat16)


def flipped(a, b, n):
    total = 0
    bit = 1
    while bit < n:
        total = total + (a // bit + b // bit) % 2 * bit
        bit *= 2
    return total


def mm(left, right):
    return jnp.dot(left, right, preferred_element_type=F32)


def kernel(
    n,
    dates,
    most,
    capacity,
    owner_ref,
    slot_ref,
    kinds_ref,
    echo_hbm,
    rref_hbm,
    aref_hbm,
    t1_hbm,
    tw_hbm,
    w2_hbm,
    pf_hbm,
    pb_hbm,
    kt_hbm,
    gfl_hbm,
    gfr_hbm,
    gbl_hbm,
    gbr_hbm,
    fil_hbm,
    entry_ref,
    echo_ref,
    rref_ref,
    t1_ref,
    tw_ref,
    w2_ref,
    pf_ref,
    pb_ref,
    kt_ref,
    gfl_ref,
    gfr_ref,
    gbl_ref,
    gbr_ref,
    ats,
    fil,
    tile_ref,
    kind_ref,
    row_ref,
    lhs,
    mat,
    snd,
    mix,
    xch,
    xin,
    azin,
    azm,
    azf,
    azx0,
    azx1,
    azx2,
    img,
    inbox,
    ybox,
    xbox,
    si,
    sa,
    sw,
    se,
    re,
    sd,
    rd,
    sz,
    rz,
    saz,
    raz,
    sf,
    rf,
    sy,
    ry,
    sx,
    rx,
):
    me = lax.axis_index("shard")
    day = lax.axis_index("date")
    grp = lax.axis_index("grp")
    relay = dates == 4
    parity = lax.rem(day, 2)
    ydst = lax.rem(day + dates - 2, dates)
    xnext = lax.rem(day + dates - 1, dates)
    xdst = day + 1 - 2 * parity if relay else xnext
    mesh_id = pl.DeviceIdType.MESH

    barrier = pltpu.get_barrier_semaphore()

    def greet(k, _):
        pl.semaphore_signal(
            barrier, inc=1, device_id=(grp, day, flipped(me, k, n)), device_id_type=mesh_id
        )
        return 0

    lax.fori_loop(1, n, greet, 0)
    if relay:
        others = [flipped(day, x, dates) for x in range(1, dates)]
    else:
        others = [lax.rem(day + 2, dates), lax.rem(day + 1, dates)]
    for other in others:
        pl.semaphore_signal(barrier, inc=1, device_id=(grp, other, me), device_id_type=mesh_id)

    pulses = echo_ref.shape[1]
    rng = echo_ref.shape[2]
    tiles = rng // BLK
    inner = rng // BLK
    mine = tiles // n
    wide = n * pulses
    rows_of = wide // BLK
    chips = n // 2
    total = n * most
    per = owner_ref.shape[1] // n
    parts = azin.shape[1]
    part = wide // parts
    near = list(range(1, chips // 2 if relay else chips))
    far = list(range(chips // 2, chips)) if relay else []

    loads = [
        pltpu.make_async_copy(a, b, si.at[i])
        for i, (a, b) in enumerate(
            [
                (echo_hbm, echo_ref),
                (rref_hbm, rref_ref),
                (t1_hbm, t1_ref),
                (tw_hbm, tw_ref),
                (w2_hbm, w2_ref),
                (pf_hbm, pf_ref),
                (pb_hbm, pb_ref),
                (kt_hbm, kt_ref),
                (gfl_hbm, gfl_ref),
                (gfr_hbm, gfr_ref),
                (gbl_hbm, gbl_ref),
                (gbr_hbm, gbr_ref),
            ]
        )
    ]
    slabs = [
        pltpu.make_async_copy(aref_hbm.at[:, :, pl.ds(t * BLK, BLK)], ats.at[t], sa.at[t])
        for t in range(mine)
    ]
    for load in loads[:5] + slabs + loads[5:]:
        load.start()

    def sources(i, _):
        dest = flipped(me, i // n, n)
        group = flipped(dest, lax.rem(i, n), n)
        seen = jnp.int32(0)
        found = [jnp.int32(0)] * most
        for b in range(per):
            named = owner_ref[0, group * per + b] == dest
            for r in range(most):
                found[r] = jnp.where(named & (seen == r), b, found[r])
            seen = seen + named.astype(jnp.int32)
        for r in range(most):
            tile_ref[i * most + r] = group * mine + lax.rem(found[r], mine)
            row_ref[i * most + r] = found[r] // mine
            kind_ref[i * most + r] = kinds_ref[0, group * per + found[r]]
        return 0

    lax.fori_loop(0, n * n, sources, 0)

    def entries(t, held):
        held = list(held)
        at = flipped(me, t, n) * most
        for b in range(per):
            named = owner_ref[0, t * per + b] == me
            slot = jnp.where(named, slot_ref[0, t * per + b], -1)
            for q in range(capacity):
                held[q] = jnp.where(slot == q, at, held[q])
            at = at + named.astype(jnp.int32)
        return tuple(held)

    for load in loads[:5]:
        load.wait()
    real = echo_ref[0].astype(F32)
    imag = echo_ref[1].astype(F32)
    rre = rref_ref[0:1, :]
    rim = rref_ref[1:2, :]
    mat[0] = (real * rre + imag * rim).reshape(pulses, tiles, BLK)
    mat[1] = (imag * rre - real * rim).reshape(pulses, tiles, BLK)

    for p in range(pulses):
        both = jnp.concatenate([mat[0, p], mat[1, p]], axis=0).T
        low = BLK // inner
        pieces = [both[x * inner : (x + 1) * inner] for x in range(low)]
        lhs[p * inner : (p + 1) * inner, :] = jnp.concatenate(pieces, axis=1).astype(BF)

    twc = tw_ref[0]
    tws = tw_ref[1]
    group = 4
    for g in range(0, pulses, group):
        section = mm(lhs[g * inner : (g + group) * inner, :], t1_ref[...])
        rights = []
        for p in range(group):
            sre = section[p * inner : (p + 1) * inner, :BLK]
            sim = section[p * inner : (p + 1) * inner, BLK:]
            rights.append(
                jnp.concatenate([sre * twc - sim * tws, sre * tws + sim * twc], axis=0).astype(BF)
            )
        second = mm(w2_ref[...], jnp.concatenate(rights, axis=1))
        for p in range(group):
            mat[:, g + p] = second[:, p * BLK : (p + 1) * BLK].reshape(2, tiles, BLK)
    for c in range(2):
        snd[c] = jnp.swapaxes(mat[c], 0, 1).astype(BF)

    def gather(k, _):
        for zz in range(chips):
            for cc in range(2):
                for r in range(most):
                    piece = snd[:, tile_ref[((2 * zz + cc) * n + k) * most + r]]
                    if cc:
                        xch[zz, k, r] = piece
                    elif zz:
                        mix[0, zz - 1, k, r] = piece
                    else:
                        xin[k, 0, r] = piece
        return 0

    lax.fori_loop(0, n, gather, 0)

    for slab in slabs:
        slab.wait()

    def filters(j, r):
        return ats.at[tile_ref[(j * n + j) * most + r] - me * mine]

    for r in range(most):
        for d in range(parts):
            rows = slice(d * part, (d + 1) * part)
            azin[0, d, r] = filters(0, r)[:, rows]
            azx0[d, r] = filters(1, r)[:, rows]
            for i, zz in enumerate(near):
                azm[0, i, d, r] = filters(2 * zz, r)[:, rows]
                azx1[i, d, r] = filters(2 * zz + 1, r)[:, rows]
        for i, zz in enumerate(far):
            rows = pl.ds(pl.multiple_of(day * part, part), part)
            azf[0, i, r] = filters(2 * zz, r)[:, rows]
            azx2[i, r] = filters(2 * zz + 1, r)[:, rows]

    pl.semaphore_wait(barrier, n - 1 + len(others))

    def remote(src, dst, send, recv, to_day, flip):
        return pltpu.make_async_remote_copy(
            src_ref=src,
            dst_ref=dst,
            send_sem=send,
            recv_sem=recv,
            device_id=(grp, to_day, me if flip is None else flipped(me, flip, n)),
            device_id_type=mesh_id,
        )

    swaps = [
        remote(xch.at[pl.ds(1, chips - 1)], mix.at[1], se.at[0], re.at[0], day, 1),
        remote(xch.at[0], xin.at[:, 1], se.at[1], re.at[1], day, 1),
        remote(azx0, azin.at[1], se.at[2], re.at[2], day, 1),
        remote(azx1, azm.at[1], se.at[3], re.at[3], day, 1),
    ]
    if far:
        swaps.append(remote(azx2, azf.at[1], se.at[4], re.at[4], day, 1))

    def direct(zz, cc):
        i = 2 * (zz - 1) + cc
        src = xch.at[zz, 0] if cc else mix.at[0, zz - 1, 0]
        return remote(src, xin.at[0, 2 * zz + cc], sd.at[i], rd.at[i], day, 2 * zz + cc)

    def step(k, zz):
        return remote(
            mix.at[:, zz - 1, k],
            xin.at[k, pl.ds(2 * zz, 2)],
            sz.at[k, zz - 1],
            rz.at[k, zz - 1],
            day,
            2 * zz,
        )

    def last(r, zz):
        return remote(
            mix.at[:, zz - 1, n - 1, r],
            xin.at[n - 1, pl.ds(2 * zz, 2), r],
            sz.at[n - 1 + r, zz - 1],
            rz.at[n - 1 + r, zz - 1],
            day,
            2 * zz,
        )

    def near_filter(i):
        zz = near[i]
        return remote(
            azm.at[:, i], azin.at[pl.ds(2 * zz, 2)], saz.at[zz - 1], raz.at[zz - 1], day, 2 * zz
        )

    def far_filter(i):
        zz = far[i]
        return remote(
            azf.at[:, i],
            azin.at[pl.ds(2 * zz, 2), day],
            saz.at[zz - 1],
            raz.at[zz - 1],
            day,
            2 * zz,
        )

    def pass_on(x):
        slab = azin.at[pl.ds(n // 2, n // 2), day]
        return remote(slab, slab, sf.at[x - 1], rf.at[x - 1], flipped(day, x, dates), None)

    swaps[0].start()
    swaps[1].start()
    for zz in range(chips - 1, 0, -1):
        for cc in range(2):
            direct(zz, cc).start()
    for swap in swaps[2:]:
        swap.start()
    swaps[0].wait_recv()
    for zz in range(chips - 1, 0, -1):
        step(1, zz).start()
    for swap in swaps[3:]:
        swap.wait_recv()
    for i in range(len(far)):
        far_filter(i).start()
    for i in range(len(near)):
        near_filter(i).start()

    def start_step(k, _):
        for zz in range(chips - 1, 0, -1):
            step(k, zz).start()
        return 0

    lax.fori_loop(2, n - 1, start_step, 0)
    for r in range(most):
        for zz in range(chips - 1, 0, -1):
            last(r, zz).start()

    held = lax.fori_loop(0, n, entries, (jnp.int32(total),) * capacity)
    for q in range(capacity):
        entry_ref[q] = held[q]
    fil[total] = jnp.zeros_like(fil[total])

    def write(e):
        return pltpu.make_async_copy(fil.at[e], fil_hbm.at[e], sw.at[e])

    write(total).start()
    for load in loads[5:]:
        load.wait()

    def copy_y(e):
        return remote(inbox.at[e], ybox.at[e], sy.at[e], ry.at[e], ydst, None)

    def copy_x(e, source, to):
        return remote(source.at[e], xbox.at[e], sx.at[e], rx.at[e], to, None)

    def focus(k, picks):
        columns = []
        filt = []
        for r in picks:
            pieces = [
                xin[k, flipped(me, s, n), r, c] for c in range(2) for s in range(n)
            ]
            columns.append(jnp.concatenate(pieces, axis=0))
            filt.append(
                [
                    jnp.concatenate([azin[k, d, r, c] for d in range(parts)], axis=0)
                    for c in range(2)
                ]
            )
        doppler = mm(pf_ref[...], jnp.concatenate(columns, axis=1))
        are = jnp.concatenate([f[0] for f in filt], axis=1).astype(F32)
        aim = jnp.concatenate([f[1] for f in filt], axis=1).astype(F32)
        dre = doppler[:wide]
        dim = doppler[wide:]
        shaped = jnp.concatenate([dre * are - dim * aim, dre * aim + dim * are], axis=0).astype(BF)
        image = mm(pb_ref[...], shaped).astype(BF)
        for i, r in enumerate(picks):
            e = k * most + r
            block = [
                jnp.concatenate(
                    [
                        image[c * wide + y * BLK : c * wide + (y + 1) * BLK, i * BLK : (i + 1) * BLK]
                        for c in range(2)
                    ],
                    axis=1,
                )
                for y in range(rows_of)
            ]
            if rows_of > 1:
                for y in range(rows_of):
                    img[i, y] = block[y]
                block = [img[i, row_ref[e]]]
            inbox[e] = mm(kt_ref[kind_ref[e]], block[0]).astype(BF)

    def stage_a(k):
        @pl.when(k == 0)
        def _():
            swaps[1].wait_recv()
            for zz in range(1, chips):
                for cc in range(2):
                    direct(zz, cc).wait_recv()

        @pl.when(k > 0)
        def _():
            for zz in range(1, chips):
                step(k, zz).wait_recv()

        @pl.when(k == 1)
        def _():
            swaps[2].wait_recv()

        for i, zz in enumerate(near):

            @pl.when(k == 2 * zz)
            def _():
                near_filter(i).wait_recv()

        if far:

            @pl.when(k == n // 2)
            def _():
                for x in range(1, dates):
                    pass_on(x).wait_recv()

        focus(k, range(most))
        for r in range(most):
            e = k * most + r
            copy_y(e).start()
            if relay:

                @pl.when(parity == 1)
                def _():
                    copy_x(e, inbox, xdst).start()
            else:
                copy_x(e, inbox, xdst).start()

    def stage_b(e):
        copy_y(e).wait_recv()
        if relay:

            @pl.when(parity == 0)
            def _():
                copy_x(e, ybox, xdst).start()

    def patches(at):
        own = inbox[at].astype(F32)
        ore = own[:, :BLK]
        oim = own[:, BLK:]
        tops = []
        lows = []
        for box in (xbox, ybox):
            oth = box[at].astype(F32)
            tre = oth[:, :BLK]
            tim = oth[:, BLK:]
            tops.append(ore * tre + oim * tim)
            lows.append(oim * tre - ore * tim)
        pair = jnp.concatenate(
            [jnp.concatenate(tops, axis=1), jnp.concatenate(lows, axis=1)], axis=0
        ).astype(BF)

        def turned(x):
            return jnp.concatenate(
                [
                    jnp.concatenate([x[:BLK, :BLK], x[BLK:, :BLK]], axis=1),
                    jnp.concatenate([x[:BLK, BLK:], x[BLK:, BLK:]], axis=1),
                ],
                axis=0,
            )

        rows = mm(gfl_ref[...], pair).astype(BF)
        spectrum = mm(turned(rows), gfr_ref[...])
        weighted = []
        for x in range(2):
            spec = spectrum[x * BLK : (x + 1) * BLK]
            sre = spec[:, :BLK]
            sim = spec[:, BLK:]
            power = sre * sre + sim * sim
            line = power + pltpu.roll(power, 1, 1) + pltpu.roll(power, BLK - 1, 1)
            smooth = (line + pltpu.roll(line, 1, 0) + pltpu.roll(line, BLK - 1, 0)) * (1.0 / 9.0)
            level = jnp.sum(jnp.sum(smooth, axis=0, keepdims=True), axis=1, keepdims=True)
            level = level * (1.0 / (BLK * BLK)) + 1e-06
            weight = lax.rsqrt(lax.rsqrt(smooth * (1.0 / level)))
            weighted.append(jnp.concatenate([sre * weight, sim * weight], axis=1))
        weighted = jnp.concatenate(weighted, axis=0).astype(BF)
        back = mm(gbl_ref[...], turned(weighted)).astype(BF)
        done = mm(turned(back), gbr_ref[...]).astype(BF)
        for x in range(2):
            for c in range(2):
                fil[at, x, c] = done[x * BLK : (x + 1) * BLK, c * BLK : (c + 1) * BLK]

    def stage_c(e):
        copy_x(e, inbox, xdst).wait_recv()
        patches(e)
        write(e).start()

    def many(stage, first, stop):
        def one(e, _):
            stage(e)
            return 0

        lax.fori_loop(first, stop, one, 0)

    def main(t, _):
        stage_a(t)

        @pl.when(t > 2)
        def _():
            stage_c((t - 3) * most)

        @pl.when(t > 0)
        def _():
            for r in range(most):
                stage_b((t - 1) * most + r)

        if far:

            @pl.when(t == 1)
            def _():
                for i in range(len(far)):
                    far_filter(i).wait_recv()
                for x in range(1, dates):
                    pass_on(x).start()

        @pl.when(t > 2)
        def _():
            many(stage_c, (t - 3) * most + 1, (t - 2) * most)

        return 0

    lax.fori_loop(0, n - 1, main, 0)
    for r in range(most):
        for zz in range(1, chips):
            last(r, zz).wait_recv()
        focus(n - 1, [r])
        e = (n - 1) * most + r
        copy_y(e).start()
        copy_x(e, inbox, xnext).start()

    def closing(r, _):
        stage_c((n - 4) * most + r)
        stage_b((n - 2) * most + r)
        return 0

    lax.fori_loop(0, most, closing, 0)
    many(stage_c, (n - 3) * most, (n - 1) * most)

    def final(e):
        copy_y(e).wait_recv()
        stage_c(e)

    many(final, (n - 1) * most, total)

    def drain(k, _):
        copy_y(k).wait_send()
        copy_x(k, inbox, xdst).wait_send()
        return 0

    for swap in swaps:
        swap.wait_send()
    for zz in range(1, chips):
        for cc in range(2):
            direct(zz, cc).wait_send()
        for r in range(most):
            last(r, zz).wait_send()

    def drain_step(k, _):
        for zz in range(1, chips):
            step(k, zz).wait_send()
        return 0

    lax.fori_loop(1, n - 1, drain_step, 0)
    for i in range(len(near)):
        near_filter(i).wait_send()
    for i in range(len(far)):
        far_filter(i).wait_send()
    if far:
        for x in range(1, dates):
            pass_on(x).wait_send()
    lax.fori_loop(0, total, drain, 0)

    def written(k, _):
        write(k).wait()
        return 0

    lax.fori_loop(0, total + 1, written, 0)


def place(capacity, entry_ref, fil_hbm, out_ref, fil, reads, sems):
    def read(q):
        return pltpu.make_async_copy(fil_hbm.at[entry_ref[q]], fil.at[q], reads.at[q])

    def copy(q):
        return pltpu.make_async_copy(fil.at[q], out_ref.at[q], sems.at[q])

    for q in range(capacity):
        read(q).start()
    for q in range(capacity):
        read(q).wait()
        copy(q).start()
    for q in range(capacity):
        copy(q).wait()


def body(dates, echo_spectra, range_reference, azimuth_reference, block_owner, block_slot, kernel_index):
    n = lax.axis_size("shard")
    per = block_owner.shape[1] // n
    most = max(2, 2 * per // n)
    capacity = min(2 * per, n * most)
    echo = echo_spectra[0]
    pulses, rng = echo.shape[1:]
    inner = rng // BLK
    mine = rng // BLK // n
    wide = pulses * n
    chips = n // 2
    relay = dates == 4
    parts = dates if relay else 1
    part = wide // parts
    near = (chips // 2 if relay else chips) - 1
    far = chips - 1 - near
    tables = [
        first_table(rng),
        twiddle_table(rng),
        left_table(inner, 1),
        left_table(wide, -1),
        left_table(wide, 1),
        kernel_table(),
        left_table(BLK, -1),
        right_table(BLK, -1),
        left_table(BLK, 1),
        right_table(BLK, 1),
    ]
    smem = pl.BlockSpec(memory_space=pltpu.SMEM)
    hbm = pl.BlockSpec(memory_space=pl.ANY)
    total = n * most
    box = pltpu.VMEM((total, BLK, 2 * BLK), BF)
    dma = pltpu.SemaphoreType.DMA
    tables = [jnp.asarray(t) for t in tables]
    operands = [block_owner, block_slot, kernel_index, echo, range_reference, azimuth_reference]
    operands += tables
    held = [echo, range_reference] + tables
    filtered, entry = pl.pallas_call(
        functools.partial(kernel, n, dates, most, capacity),
        out_shape=(
            jax.ShapeDtypeStruct((total + 1, 2, 2, BLK, BLK), BF),
            jax.ShapeDtypeStruct((capacity,), jnp.int32),
        ),
        in_specs=[smem] * 3 + [hbm] * 13,
        out_specs=(hbm, smem),
        scratch_shapes=[pltpu.VMEM(a.shape, a.dtype) for a in held]
        + [
            pltpu.VMEM((mine, 2, wide, BLK), BF),
            pltpu.VMEM((total + 1, 2, 2, BLK, BLK), BF),
            pltpu.SMEM((n * total,), jnp.int32),
            pltpu.SMEM((n * total,), jnp.int32),
            pltpu.SMEM((n * total,), jnp.int32),
            pltpu.VMEM((pulses * inner, 2 * BLK), BF),
            pltpu.VMEM((2, pulses, rng // BLK, BLK), F32),
            pltpu.VMEM((2, rng // BLK, pulses, BLK), BF),
            pltpu.VMEM((2, chips - 1, n, most, 2, pulses, BLK), BF),
            pltpu.VMEM((chips, n, most, 2, pulses, BLK), BF),
            pltpu.VMEM((n, n, most, 2, pulses, BLK), BF),
            pltpu.VMEM((n, parts, most, 2, part, BLK), BF),
            pltpu.VMEM((2, near, parts, most, 2, part, BLK), BF),
            pltpu.VMEM((2, max(far, 1), most, 2, part, BLK), BF),
            pltpu.VMEM((parts, most, 2, part, BLK), BF),
            pltpu.VMEM((near, parts, most, 2, part, BLK), BF),
            pltpu.VMEM((max(far, 1), most, 2, part, BLK), BF),
            pltpu.VMEM((most, wide // BLK, BLK, 2 * BLK), BF),
            box,
            box,
            box,
            dma((len(held),)),
            dma((mine,)),
            dma((total + 1,)),
            *[dma((5,))] * 2,
            *[dma((2 * (chips - 1),))] * 2,
            *[dma((n - 1 + most, chips - 1))] * 2,
            *[dma((chips - 1,))] * 2,
            *[dma((dates - 1,))] * 2,
            *[dma((total,))] * 4,
        ],
        compiler_params=pltpu.CompilerParams(collective_id=0, has_side_effects=True),
    )(
        *operands
    )
    out = pl.pallas_call(
        functools.partial(place, capacity),
        out_shape=jax.ShapeDtypeStruct((capacity, 2, 2, BLK, BLK), BF),
        in_specs=[smem, hbm],
        out_specs=hbm,
        scratch_shapes=[
            pltpu.VMEM((capacity, 2, 2, BLK, BLK), BF),
            dma((capacity,)),
            dma((capacity,)),
        ],
    )(entry, filtered)
    return out[None]


def solution(mesh):
    in_specs = (
        P(("grp", "date"), None, "shard", None),
        P(),
        P(None, None, "shard"),
        P(("grp", "date"), None),
        P(("grp", "date"), None),
        P(("grp", "date"), None),
    )
    out_specs = P(("grp", "date"), "shard", None, None, None, None)
    return jax.shard_map(
        functools.partial(body, mesh.shape["date"]),
        mesh=mesh,
        in_specs=in_specs,
        out_specs=out_specs,
        check_vma=False,
    )
```

time: 59.7 us -> 62 us (1.039)
  Pallas kernels: 58.6 us -> 61.1 us
    pallas_call x1, Pallas kernels: 55.5 us -> 57.5 us  [body(): pl.pallas_call(functools.partial(kernel, n, dates, most, capacity), out_s...]
where the time goes in v1:
time: 62 us; the launch traced here: 61.2 us
  Pallas kernels  61.1 us (99%)
    pallas_call x1, Pallas kernels, body(): pl.pallas_call(functools.partial(kernel, n, dates, most, capacity), out_s...  57.5 us
    pallas_call x1, Pallas kernels, body(): pl.pallas_call(functools.partial(place, capacity), out_shape=jax.ShapeDty...  3.61 us

profile of v1, /device:TPU:2, one launch (start us, length us, event | category | flops | bytes accessed | tf_op | source)
XLA Modules:
  0.0 61.2 jit_solution(1514230191760203816)
XLA Ops:
  0.0 57.5 %shard_map.154 = (bf16[17,2,2,128,128]{4,3,2,1,0:T(8,128)(2,1)}, s32[16]{0:T(128)}) custom-call(s32[1,64]{1,0:T(1,128)} %owner_ref.1, s32[1,64]{1,0:T(1,128)} %slot_ref.1, s32[1,64]{1,0:T(1,128)} %kinds_ref.1, bf16[2,16,8192]{2,1,0:T(8,128)(2,1)} %bitcast.2, f32[2,8192]{1,0:T(2,128)} %rref_hbm.1, bf16[2,128,1024]{2,1,0:T(8,128)(2,1)} %aref_hbm.1, ...), custom_call_target="tpu_custom_call" | custom-call | tf_op jit(solution)/shard_map/pallas_call | solution.py:706
  57.5 3.6 %shard_map.155 = bf16[16,2,2,128,128]{4,3,2,1,0:T(8,128)(2,1)} custom-call(s32[16]{0:T(128)} %get-tuple-element.7.entry_ref, bf16[17,2,2,128,128]{4,3,2,1,0:T(8,128)(2,1)} %get-tuple-element.8.fil_hbm), custom_call_target="tpu_custom_call" | custom-call | tf_op jit(solution)/shard_map/pallas_call | solution.py:751

commit v2 on v1

--- a/solution.py
+++ b/solution.py
@@ -12,6 +12,7 @@
 
 BLK = 128
 NSUB = 8
+WORD = 4
 BF = jnp.bfloat16
 F32 = jnp.float32
 
@@ -90,7 +91,7 @@
     gfr_hbm,
     gbl_hbm,
     gbr_hbm,
-    fil_hbm,
+    fil,
     entry_ref,
     echo_ref,
     rref_ref,
@@ -105,7 +106,6 @@
     gbl_ref,
     gbr_ref,
     ats,
-    fil,
     tile_ref,
     kind_ref,
     row_ref,
@@ -127,7 +127,6 @@
     xbox,
     si,
     sa,
-    sw,
     se,
     re,
     sd,
@@ -210,27 +209,48 @@
     for load in loads[:5] + slabs + loads[5:]:
         load.start()
 
-    def sources(i, _):
-        dest = flipped(me, i // n, n)
-        group = flipped(dest, lax.rem(i, n), n)
+    bits = 32 // WORD
+    words = (n + bits - 1) // bits
+
+    def sources(g, _):
+        packed = [[jnp.int32(0)] * most for _ in range(words)]
+        for b in range(per):
+            owner = owner_ref[0, g * per + b]
+            for w in range(words):
+                shift = (owner - w * bits) * WORD
+                live = None
+                if words > 1:
+                    live = owner // bits == w
+                    shift = jnp.where(live, shift, 0)
+                for r in range(most):
+                    empty = ((packed[w][r] >> shift) & (2**WORD - 1)) == 0
+                    put = empty if live is None else live & empty
+                    packed[w][r] = packed[w][r] | jnp.where(put, (b + 1) << shift, 0)
+                    live = ~empty if live is None else live & ~empty
+        for w in range(words):
+            for x in range(w * bits, min(n, (w + 1) * bits)):
+                flip = flipped(me, x, n)
+                for r in range(most):
+                    found = (packed[w][r] >> ((x - w * bits) * WORD)) & (2**WORD - 1)
+                    found = jnp.maximum(found - 1, 0)
+                    tile_ref[(flip * n + flipped(g, x, n)) * most + r] = g * mine + lax.rem(found, mine)
+        return 0
+
+    lax.fori_loop(0, n, sources, 0)
+
+    def entries(t, held):
+        held = list(held)
+        at = flipped(me, t, n) * most
+        found = [jnp.int32(0)] * most
         seen = jnp.int32(0)
-        found = [jnp.int32(0)] * most
         for b in range(per):
-            named = owner_ref[0, group * per + b] == dest
+            named = owner_ref[0, t * per + b] == me
             for r in range(most):
                 found[r] = jnp.where(named & (seen == r), b, found[r])
             seen = seen + named.astype(jnp.int32)
         for r in range(most):
-            tile_ref[i * most + r] = group * mine + lax.rem(found[r], mine)
-            row_ref[i * most + r] = found[r] // mine
-            kind_ref[i * most + r] = kinds_ref[0, group * per + found[r]]
-        return 0
-
-    lax.fori_loop(0, n * n, sources, 0)
-
-    def entries(t, held):
-        held = list(held)
-        at = flipped(me, t, n) * most
+            row_ref[at + r] = found[r] // mine
+            kind_ref[at + r] = kinds_ref[0, t * per + found[r]]
         for b in range(per):
             named = owner_ref[0, t * per + b] == me
             slot = jnp.where(named, slot_ref[0, t * per + b], -1)
@@ -405,18 +425,18 @@
         entry_ref[q] = held[q]
     fil[total] = jnp.zeros_like(fil[total])
 
-    def write(e):
-        return pltpu.make_async_copy(fil.at[e], fil_hbm.at[e], sw.at[e])
-
-    write(total).start()
     for load in loads[5:]:
         load.wait()
 
-    def copy_y(e):
-        return remote(inbox.at[e], ybox.at[e], sy.at[e], ry.at[e], ydst, None)
-
-    def copy_x(e, source, to):
-        return remote(source.at[e], xbox.at[e], sx.at[e], rx.at[e], to, None)
+    joined = 0
+
+    def copy_y(e, count):
+        span = pl.ds(e, count)
+        return remote(inbox.at[span], ybox.at[span], sy.at[e], ry.at[e], ydst, None)
+
+    def copy_x(e, source, to, count):
+        span = pl.ds(e, count)
+        return remote(source.at[span], xbox.at[span], sx.at[e], rx.at[e], to, None)
 
     def focus(k, picks):
         columns = []
@@ -488,24 +508,40 @@
                     pass_on(x).wait_recv()
 
         focus(k, range(most))
-        for r in range(most):
-            e = k * most + r
-            copy_y(e).start()
+
+        def send(e, count):
+            copy_y(e, count).start()
             if relay:
 
                 @pl.when(parity == 1)
                 def _():
-                    copy_x(e, inbox, xdst).start()
+                    copy_x(e, inbox, xdst, count).start()
             else:
-                copy_x(e, inbox, xdst).start()
-
-    def stage_b(e):
-        copy_y(e).wait_recv()
-        if relay:
-
-            @pl.when(parity == 0)
+                copy_x(e, inbox, xdst, count).start()
+
+        each(k, range(most), send)
+
+    def each(k, picks, act):
+        for r in picks:
+
+            @pl.when((k < joined) & (r == 0))
             def _():
-                copy_x(e, ybox, xdst).start()
+                act(k * most, most)
+
+            @pl.when(k >= joined)
+            def _():
+                act(k * most + r, 1)
+
+    def stage_b(k, r):
+        def onward(e, count):
+            copy_y(e, count).wait_recv()
+            if relay:
+
+                @pl.when(parity == 0)
+                def _():
+                    copy_x(e, ybox, xdst, count).start()
+
+        each(k, [r], onward)
 
     def patches(at):
         own = inbox[at].astype(F32)
@@ -553,30 +589,29 @@
             for c in range(2):
                 fil[at, x, c] = done[x * BLK : (x + 1) * BLK, c * BLK : (c + 1) * BLK]
 
-    def stage_c(e):
-        copy_x(e, inbox, xdst).wait_recv()
-        patches(e)
-        write(e).start()
-
-    def many(stage, first, stop):
-        def one(e, _):
-            stage(e)
+    def stage_c(k, r):
+        each(k, [r], lambda e, count: copy_x(e, inbox, xdst, count).wait_recv())
+        patches(k * most + r)
+
+    def pace(kb, kc):
+        def one(r, _):
+            @pl.when(kb >= 0)
+            def _():
+                stage_b(kb, r)
+
+            @pl.when(kc >= 0)
+            def _():
+                stage_c(kc, r)
+
             return 0
 
-        lax.fori_loop(first, stop, one, 0)
+        lax.fori_loop(0, most, one, 0)
+
+    lag = 3
 
     def main(t, _):
         stage_a(t)
-
-        @pl.when(t > 2)
-        def _():
-            stage_c((t - 3) * most)
-
-        @pl.when(t > 0)
-        def _():
-            for r in range(most):
-                stage_b((t - 1) * most + r)
-
+        pace(t - 1, t - lag)
         if far:
 
             @pl.when(t == 1)
@@ -586,10 +621,6 @@
                 for x in range(1, dates):
                     pass_on(x).start()
 
-        @pl.when(t > 2)
-        def _():
-            many(stage_c, (t - 3) * most + 1, (t - 2) * most)
-
         return 0
 
     lax.fori_loop(0, n - 1, main, 0)
@@ -598,26 +629,29 @@
             last(r, zz).wait_recv()
         focus(n - 1, [r])
         e = (n - 1) * most + r
-        copy_y(e).start()
-        copy_x(e, inbox, xnext).start()
-
-    def closing(r, _):
-        stage_c((n - 4) * most + r)
-        stage_b((n - 2) * most + r)
+        copy_y(e, 1).start()
+        copy_x(e, inbox, xnext, 1).start()
+    pace(n - 2, n - 1 - lag)
+
+    def closing(i, _):
+        k = n - lag + i // most
+        r = lax.rem(i, most)
+
+        @pl.when(k == n - 1)
+        def _():
+            copy_y(k * most + r, 1).wait_recv()
+
+        stage_c(k, r)
         return 0
 
-    lax.fori_loop(0, most, closing, 0)
-    many(stage_c, (n - 3) * most, (n - 1) * most)
-
-    def final(e):
-        copy_y(e).wait_recv()
-        stage_c(e)
-
-    many(final, (n - 1) * most, total)
+    lax.fori_loop(0, lag * most, closing, 0)
+
+    def sent(e, count):
+        copy_y(e, count).wait_send()
+        copy_x(e, inbox, xdst, count).wait_send()
 
     def drain(k, _):
-        copy_y(k).wait_send()
-        copy_x(k, inbox, xdst).wait_send()
+        each(k, range(most), sent)
         return 0
 
     for swap in swaps:
@@ -641,26 +675,14 @@
     if far:
         for x in range(1, dates):
             pass_on(x).wait_send()
-    lax.fori_loop(0, total, drain, 0)
-
-    def written(k, _):
-        write(k).wait()
-        return 0
-
-    lax.fori_loop(0, total + 1, written, 0)
-
-
-def place(capacity, entry_ref, fil_hbm, out_ref, fil, reads, sems):
-    def read(q):
-        return pltpu.make_async_copy(fil_hbm.at[entry_ref[q]], fil.at[q], reads.at[q])
-
+    lax.fori_loop(0, n, drain, 0)
+
+
+def place(capacity, entry_ref, fil, out_ref, sems):
     def copy(q):
-        return pltpu.make_async_copy(fil.at[q], out_ref.at[q], sems.at[q])
+        return pltpu.make_async_copy(fil.at[entry_ref[q]], out_ref.at[q], sems.at[q])
 
     for q in range(capacity):
-        read(q).start()
-    for q in range(capacity):
-        read(q).wait()
         copy(q).start()
     for q in range(capacity):
         copy(q).wait()
@@ -696,8 +718,10 @@
     ]
     smem = pl.BlockSpec(memory_space=pltpu.SMEM)
     hbm = pl.BlockSpec(memory_space=pl.ANY)
+    vmem = pl.BlockSpec(memory_space=pltpu.VMEM)
     total = n * most
     box = pltpu.VMEM((total, BLK, 2 * BLK), BF)
+    grant = min(60 * 1024 * 1024, 63 * 2**20 - (total + 2) * 4 * BLK * BLK * 2)
     dma = pltpu.SemaphoreType.DMA
     tables = [jnp.asarray(t) for t in tables]
     operands = [block_owner, block_slot, kernel_index, echo, range_reference, azimuth_reference]
@@ -706,18 +730,17 @@
     filtered, entry = pl.pallas_call(
         functools.partial(kernel, n, dates, most, capacity),
         out_shape=(
-            jax.ShapeDtypeStruct((total + 1, 2, 2, BLK, BLK), BF),
+            pltpu.VMEM((total + 1, 2, 2, BLK, BLK), BF),
             jax.ShapeDtypeStruct((capacity,), jnp.int32),
         ),
         in_specs=[smem] * 3 + [hbm] * 13,
-        out_specs=(hbm, smem),
+        out_specs=(vmem, smem),
         scratch_shapes=[pltpu.VMEM(a.shape, a.dtype) for a in held]
         + [
             pltpu.VMEM((mine, 2, wide, BLK), BF),
-            pltpu.VMEM((total + 1, 2, 2, BLK, BLK), BF),
             pltpu.SMEM((n * total,), jnp.int32),
-            pltpu.SMEM((n * total,), jnp.int32),
-            pltpu.SMEM((n * total,), jnp.int32),
+            pltpu.SMEM((total,), jnp.int32),
+            pltpu.SMEM((total,), jnp.int32),
             pltpu.VMEM((pulses * inner, 2 * BLK), BF),
             pltpu.VMEM((2, pulses, rng // BLK, BLK), F32),
             pltpu.VMEM((2, rng // BLK, pulses, BLK), BF),
@@ -736,7 +759,6 @@
             box,
             dma((len(held),)),
             dma((mine,)),
-            dma((total + 1,)),
             *[dma((5,))] * 2,
             *[dma((2 * (chips - 1),))] * 2,
             *[dma((n - 1 + most, chips - 1))] * 2,
@@ -744,21 +766,20 @@
             *[dma((dates - 1,))] * 2,
             *[dma((total,))] * 4,
         ],
-        compiler_params=pltpu.CompilerParams(collective_id=0, has_side_effects=True),
+        compiler_params=pltpu.CompilerParams(
+            collective_id=0, has_side_effects=True, vmem_limit_bytes=grant
+        ),
     )(
         *operands
     )
     out = pl.pallas_call(
         functools.partial(place, capacity),
         out_shape=jax.ShapeDtypeStruct((capacity, 2, 2, BLK, BLK), BF),
-        in_specs=[smem, hbm],
+        in_specs=[smem, vmem],
         out_specs=hbm,
-        scratch_shapes=[
-            pltpu.VMEM((capacity, 2, 2, BLK, BLK), BF),
-            dma((capacity,)),
-            dma((capacity,)),
-        ],
-    )(entry, filtered)
+        scratch_shapes=[dma((capacity,))],
+        compiler_params=pltpu.CompilerParams(vmem_limit_bytes=grant),
+    )(entry, pltpu.with_memory_space_constraint(filtered, pltpu.VMEM))
     return out[None]
 
 

time: 62 us -> 55 us (0.89)
  Pallas kernels: 61.1 us -> 54.6 us
    pallas_call x1, Pallas kernels: 57.5 us -> 52.5 us  [body(): pl.pallas_call(functools.partial(kernel, n, dates, most, capacity), out_s...]
    pallas_call x1, Pallas kernels: 3.61 us -> 2.1 us  [body(): pl.pallas_call(functools.partial(place, capacity), out_shape=jax.ShapeDty...]
where the time goes in v2:
time: 55 us; the launch traced here: 54.6 us
  Pallas kernels  54.6 us (99%)
    pallas_call x1, Pallas kernels, body(): pl.pallas_call(functools.partial(kernel, n, dates, most, capacity), out_s...  52.5 us
    pallas_call x1, Pallas kernels, body(): pl.pallas_call(functools.partial(place, capacity), out_shape=jax.ShapeDty...  2.1 us

profile of v2, /device:TPU:2, one launch (start us, length us, event | category | flops | bytes accessed | tf_op | source)
XLA Modules:
  0.0 54.6 jit_solution(13110859067307928462)
XLA Ops:
  0.0 52.5 %shard_map.154 = (bf16[17,2,2,128,128]{4,3,2,1,0:T(8,128)(2,1)S(1)}, s32[16]{0:T(128)}) custom-call(s32[1,64]{1,0:T(1,128)} %owner_ref.1, s32[1,64]{1,0:T(1,128)} %slot_ref.1, s32[1,64]{1,0:T(1,128)} %kinds_ref.1, bf16[2,16,8192]{2,1,0:T(8,128)(2,1)} %bitcast.2, f32[2,8192]{1,0:T(2,128)} %rref_hbm.1, bf16[2,128,1024]{2,1,0:T(8,128)(2,1)} %aref_hbm.1, ...), custom_call_target="tpu_custom_call" | custom-call | tf_op jit(solution)/shard_map/pallas_call | solution.py:730
  52.5 2.1 %shard_map.155 = bf16[16,2,2,128,128]{4,3,2,1,0:T(8,128)(2,1)} custom-call(s32[16]{0:T(128)} %get-tuple-element.7.entry_ref, bf16[17,2,2,128,128]{4,3,2,1,0:T(8,128)(2,1)S(1)} %get-tuple-element.8.fil), custom_call_target="tpu_custom_call" | custom-call | tf_op jit(solution)/shard_map/pallas_call | solution.py:775

commit v3 on v2

--- a/solution.py
+++ b/solution.py
@@ -92,7 +92,9 @@
     gbl_hbm,
     gbr_hbm,
     fil,
+    entry_out,
     entry_ref,
+    sl,
     echo_ref,
     rref_ref,
     t1_ref,
@@ -393,20 +395,25 @@
         slab = azin.at[pl.ds(n // 2, n // 2), day]
         return remote(slab, slab, sf.at[x - 1], rf.at[x - 1], flipped(day, x, dates), None)
 
-    swaps[0].start()
-    swaps[1].start()
+    def pass_far(x, held):
+        half = azin.at[pl.ds(n // 2 + (2 - x) * (n // 4), n // 4), held]
+        return remote(half, half, sf.at[x + 1], rf.at[x + 1], flipped(day, x, dates), None)
+
+    for swap in [swaps[1]] + swaps[4:] + swaps[:1]:
+        swap.start()
     for zz in range(chips - 1, 0, -1):
         for cc in range(2):
             direct(zz, cc).start()
-    for swap in swaps[2:]:
+    for swap in swaps[2:4]:
         swap.start()
+    for swap in swaps[4:]:
+        swap.wait_recv()
+    for i in range(len(far)):
+        far_filter(i).start()
     swaps[0].wait_recv()
     for zz in range(chips - 1, 0, -1):
         step(1, zz).start()
-    for swap in swaps[3:]:
-        swap.wait_recv()
-    for i in range(len(far)):
-        far_filter(i).start()
+    swaps[3].wait_recv()
     for i in range(len(near)):
         near_filter(i).start()
 
@@ -423,6 +430,8 @@
     held = lax.fori_loop(0, n, entries, (jnp.int32(total),) * capacity)
     for q in range(capacity):
         entry_ref[q] = held[q]
+    list_copy = pltpu.make_async_copy(entry_ref, entry_out, sl.at[0])
+    list_copy.start()
     fil[total] = jnp.zeros_like(fil[total])
 
     for load in loads[5:]:
@@ -504,8 +513,8 @@
 
             @pl.when(k == n // 2)
             def _():
-                for x in range(1, dates):
-                    pass_on(x).wait_recv()
+                for x in (1, 2):
+                    pass_far(x, flipped(day, 3, dates)).wait_recv()
 
         focus(k, range(most))
 
@@ -607,19 +616,25 @@
 
         lax.fori_loop(0, most, one, 0)
 
-    lag = 3
+    lag = 2
 
     def main(t, _):
         stage_a(t)
         pace(t - 1, t - lag)
         if far:
 
-            @pl.when(t == 1)
+            @pl.when(t == 0)
             def _():
                 for i in range(len(far)):
                     far_filter(i).wait_recv()
-                for x in range(1, dates):
+                for x in (1, 2):
                     pass_on(x).start()
+
+            @pl.when(t == 1)
+            def _():
+                for x in (1, 2):
+                    pass_on(3 - x).wait_recv()
+                    pass_far(x, flipped(day, 3 - x, dates)).start()
 
         return 0
 
@@ -630,14 +645,24 @@
         focus(n - 1, [r])
         e = (n - 1) * most + r
         copy_y(e, 1).start()
-        copy_x(e, inbox, xnext, 1).start()
+        if r == most - 1:
+            copy_x(e, inbox, xnext, 1).start()
+        elif relay:
+
+            @pl.when(parity == 1)
+            def _():
+                copy_x(e, inbox, xdst, 1).start()
+        else:
+            copy_x(e, inbox, xdst, 1).start()
     pace(n - 2, n - 1 - lag)
+    for r in range(most - 1):
+        stage_b(n - 1, r)
 
     def closing(i, _):
         k = n - lag + i // most
         r = lax.rem(i, most)
 
-        @pl.when(k == n - 1)
+        @pl.when((k == n - 1) & (r == most - 1))
         def _():
             copy_y(k * most + r, 1).wait_recv()
 
@@ -673,9 +698,11 @@
     for i in range(len(far)):
         far_filter(i).wait_send()
     if far:
-        for x in range(1, dates):
+        for x in (1, 2):
             pass_on(x).wait_send()
+            pass_far(x, flipped(day, 3 - x, dates)).wait_send()
     lax.fori_loop(0, n, drain, 0)
+    list_copy.wait()
 
 
 def place(capacity, entry_ref, fil, out_ref, sems):
@@ -734,8 +761,9 @@
             jax.ShapeDtypeStruct((capacity,), jnp.int32),
         ),
         in_specs=[smem] * 3 + [hbm] * 13,
-        out_specs=(vmem, smem),
-        scratch_shapes=[pltpu.VMEM(a.shape, a.dtype) for a in held]
+        out_specs=(vmem, hbm),
+        scratch_shapes=[pltpu.SMEM((capacity,), jnp.int32), dma((1,))]
+        + [pltpu.VMEM(a.shape, a.dtype) for a in held]
         + [
             pltpu.VMEM((mine, 2, wide, BLK), BF),
             pltpu.SMEM((n * total,), jnp.int32),
@@ -763,7 +791,7 @@
             *[dma((2 * (chips - 1),))] * 2,
             *[dma((n - 1 + most, chips - 1))] * 2,
             *[dma((chips - 1,))] * 2,
-            *[dma((dates - 1,))] * 2,
+            *[dma((4,))] * 2,
             *[dma((total,))] * 4,
         ],
         compiler_params=pltpu.CompilerParams(

time: 55 us -> 52.6 us (0.956)
  Pallas kernels: 54.6 us -> 52.4 us
    pallas_call x1, Pallas kernels: 52.5 us -> 50.3 us  [body(): pl.pallas_call(functools.partial(kernel, n, dates, most, capacity), out_s...]
where the time goes in v3:
time: 52.6 us; the launch traced here: 52.4 us
  Pallas kernels  52.4 us (100%)
    pallas_call x1, Pallas kernels, body(): pl.pallas_call(functools.partial(kernel, n, dates, most, capacity), out_s...  50.3 us
    pallas_call x1, Pallas kernels, body(): pl.pallas_call(functools.partial(place, capacity), out_shape=jax.ShapeDty...  2.1 us

profile of v3, /device:TPU:2, one launch (start us, length us, event | category | flops | bytes accessed | tf_op | source)
XLA Modules:
  0.0 52.4 jit_solution(3819106561027763104)
XLA Ops:
  0.0 50.3 %shard_map.154 = (bf16[17,2,2,128,128]{4,3,2,1,0:T(8,128)(2,1)S(1)}, s32[16]{0:T(128)}) custom-call(s32[1,64]{1,0:T(1,128)} %owner_ref.1, s32[1,64]{1,0:T(1,128)} %slot_ref.1, s32[1,64]{1,0:T(1,128)} %kinds_ref.1, bf16[2,16,8192]{2,1,0:T(8,128)(2,1)} %bitcast.2, f32[2,8192]{1,0:T(2,128)} %rref_hbm.1, bf16[2,128,1024]{2,1,0:T(8,128)(2,1)} %aref_hbm.1, ...), custom_call_target="tpu_custom_call" | custom-call | tf_op jit(solution)/shard_map/pallas_call | solution.py:757
  50.3 2.1 %shard_map.155 = bf16[16,2,2,128,128]{4,3,2,1,0:T(8,128)(2,1)} custom-call(s32[16]{0:T(128)} %get-tuple-element.7.entry_ref, bf16[17,2,2,128,128]{4,3,2,1,0:T(8,128)(2,1)S(1)} %get-tuple-element.8.fil), custom_call_target="tpu_custom_call" | custom-call | tf_op jit(solution)/shard_map/pallas_call | solution.py:803

commit v4 on v3

--- a/solution.py
+++ b/solution.py
@@ -304,10 +304,10 @@
                     elif zz:
                         mix[0, zz - 1, k, r] = piece
                     else:
-                        xin[k, 0, r] = piece
+                        xin[0, k, r] = piece
         return 0
 
-    lax.fori_loop(0, n, gather, 0)
+    gather(0, 0)
 
     for slab in slabs:
         slab.wait()
@@ -316,13 +316,6 @@
         return ats.at[tile_ref[(j * n + j) * most + r] - me * mine]
 
     for r in range(most):
-        for d in range(parts):
-            rows = slice(d * part, (d + 1) * part)
-            azin[0, d, r] = filters(0, r)[:, rows]
-            azx0[d, r] = filters(1, r)[:, rows]
-            for i, zz in enumerate(near):
-                azm[0, i, d, r] = filters(2 * zz, r)[:, rows]
-                azx1[i, d, r] = filters(2 * zz + 1, r)[:, rows]
         for i, zz in enumerate(far):
             rows = pl.ds(pl.multiple_of(day * part, part), part)
             azf[0, i, r] = filters(2 * zz, r)[:, rows]
@@ -342,7 +335,7 @@
 
     swaps = [
         remote(xch.at[pl.ds(1, chips - 1)], mix.at[1], se.at[0], re.at[0], day, 1),
-        remote(xch.at[0], xin.at[:, 1], se.at[1], re.at[1], day, 1),
+        remote(xch.at[0], xin.at[1], se.at[1], re.at[1], day, 1),
         remote(azx0, azin.at[1], se.at[2], re.at[2], day, 1),
         remote(azx1, azm.at[1], se.at[3], re.at[3], day, 1),
     ]
@@ -352,12 +345,13 @@
     def direct(zz, cc):
         i = 2 * (zz - 1) + cc
         src = xch.at[zz, 0] if cc else mix.at[0, zz - 1, 0]
-        return remote(src, xin.at[0, 2 * zz + cc], sd.at[i], rd.at[i], day, 2 * zz + cc)
-
-    def step(k, zz):
+        return remote(src, xin.at[2 * zz + cc, 0], sd.at[i], rd.at[i], day, 2 * zz + cc)
+
+    def step(k, zz, count=1):
+        span = pl.ds(k, count)
         return remote(
-            mix.at[:, zz - 1, k],
-            xin.at[k, pl.ds(2 * zz, 2)],
+            mix.at[:, zz - 1, span],
+            xin.at[pl.ds(2 * zz, 2), span],
             sz.at[k, zz - 1],
             rz.at[k, zz - 1],
             day,
@@ -367,7 +361,7 @@
     def last(r, zz):
         return remote(
             mix.at[:, zz - 1, n - 1, r],
-            xin.at[n - 1, pl.ds(2 * zz, 2), r],
+            xin.at[pl.ds(2 * zz, 2), n - 1, r],
             sz.at[n - 1 + r, zz - 1],
             rz.at[n - 1 + r, zz - 1],
             day,
@@ -399,11 +393,22 @@
         half = azin.at[pl.ds(n // 2 + (2 - x) * (n // 4), n // 4), held]
         return remote(half, half, sf.at[x + 1], rf.at[x + 1], flipped(day, x, dates), None)
 
-    for swap in [swaps[1]] + swaps[4:] + swaps[:1]:
-        swap.start()
     for zz in range(chips - 1, 0, -1):
         for cc in range(2):
             direct(zz, cc).start()
+    for swap in swaps[4:]:
+        swap.start()
+    lax.fori_loop(1, n, gather, 0)
+    swaps[1].start()
+    swaps[0].start()
+    for r in range(most):
+        for d in range(parts):
+            rows = slice(d * part, (d + 1) * part)
+            azin[0, d, r] = filters(0, r)[:, rows]
+            azx0[d, r] = filters(1, r)[:, rows]
+            for i, zz in enumerate(near):
+                azm[0, i, d, r] = filters(2 * zz, r)[:, rows]
+                azx1[i, d, r] = filters(2 * zz + 1, r)[:, rows]
     for swap in swaps[2:4]:
         swap.start()
     for swap in swaps[4:]:
@@ -452,7 +457,7 @@
         filt = []
         for r in picks:
             pieces = [
-                xin[k, flipped(me, s, n), r, c] for c in range(2) for s in range(n)
+                xin[flipped(me, s, n), k, r, c] for c in range(2) for s in range(n)
             ]
             columns.append(jnp.concatenate(pieces, axis=0))
             filt.append(
@@ -586,9 +591,9 @@
             sim = spec[:, BLK:]
             power = sre * sre + sim * sim
             line = power + pltpu.roll(power, 1, 1) + pltpu.roll(power, BLK - 1, 1)
-            smooth = (line + pltpu.roll(line, 1, 0) + pltpu.roll(line, BLK - 1, 0)) * (1.0 / 9.0)
-            level = jnp.sum(jnp.sum(smooth, axis=0, keepdims=True), axis=1, keepdims=True)
-            level = level * (1.0 / (BLK * BLK)) + 1e-06
+            smooth = line + pltpu.roll(line, 1, 0) + pltpu.roll(line, BLK - 1, 0)
+            level = jnp.sum(jnp.sum(power, axis=0, keepdims=True), axis=1, keepdims=True)
+            level = 9.0 * (level * (1.0 / (BLK * BLK)) + 1e-06)
             weight = lax.rsqrt(lax.rsqrt(smooth * (1.0 / level)))
             weighted.append(jnp.concatenate([sre * weight, sim * weight], axis=1))
         weighted = jnp.concatenate(weighted, axis=0).astype(BF)
@@ -604,13 +609,13 @@
 
     def pace(kb, kc):
         def one(r, _):
+            @pl.when(kc >= 0)
+            def _():
+                stage_c(kc, r)
+
             @pl.when(kb >= 0)
             def _():
                 stage_b(kb, r)
-
-            @pl.when(kc >= 0)
-            def _():
-                stage_c(kc, r)
 
             return 0
 
@@ -661,6 +666,7 @@
     def closing(i, _):
         k = n - lag + i // most
         r = lax.rem(i, most)
+        r = jnp.where(k == n - 1, most - 1 - r, r)
 
         @pl.when((k == n - 1) & (r == most - 1))
         def _():
@@ -710,7 +716,7 @@
         return pltpu.make_async_copy(fil.at[entry_ref[q]], out_ref.at[q], sems.at[q])
 
     for q in range(capacity):
-        copy(q).start()
+        copy(q).start(priority=q % 2)
     for q in range(capacity):
         copy(q).wait()
 

time: 52.6 us -> 52 us (0.989)
  Pallas kernels: 52.4 us -> 51.8 us
    pallas_call x1, Pallas kernels: 50.3 us -> 49.7 us  [body(): pl.pallas_call(functools.partial(kernel, n, dates, most, capacity), out_s...]
where the time goes in v4:
time: 52 us; the launch traced here: 51.8 us
  Pallas kernels  51.8 us (100%)
    pallas_call x1, Pallas kernels, body(): pl.pallas_call(functools.partial(kernel, n, dates, most, capacity), out_s...  49.7 us
    pallas_call x1, Pallas kernels, body(): pl.pallas_call(functools.partial(place, capacity), out_shape=jax.ShapeDty...  2.1 us

profile of v4, /device:TPU:2, one launch (start us, length us, event | category | flops | bytes accessed | tf_op | source)
XLA Modules:
  0.0 51.8 jit_solution(6934572548482884838)
XLA Ops:
  0.0 49.7 %shard_map.154 = (bf16[17,2,2,128,128]{4,3,2,1,0:T(8,128)(2,1)S(1)}, s32[16]{0:T(128)}) custom-call(s32[1,64]{1,0:T(1,128)} %owner_ref.1, s32[1,64]{1,0:T(1,128)} %slot_ref.1, s32[1,64]{1,0:T(1,128)} %kinds_ref.1, bf16[2,16,8192]{2,1,0:T(8,128)(2,1)} %bitcast.2, f32[2,8192]{1,0:T(2,128)} %rref_hbm.1, bf16[2,128,1024]{2,1,0:T(8,128)(2,1)} %aref_hbm.1, ...), custom_call_target="tpu_custom_call" | custom-call | tf_op jit(solution)/shard_map/pallas_call | solution.py:763
  49.7 2.1 %shard_map.155 = bf16[16,2,2,128,128]{4,3,2,1,0:T(8,128)(2,1)} custom-call(s32[16]{0:T(128)} %get-tuple-element.7.entry_ref, bf16[17,2,2,128,128]{4,3,2,1,0:T(8,128)(2,1)S(1)} %get-tuple-element.8.fil), custom_call_target="tpu_custom_call" | custom-call | tf_op jit(solution)/shard_map/pallas_call | solution.py:809

commit v5 on v4

--- a/solution.py
+++ b/solution.py
@@ -158,7 +158,7 @@
 
     def greet(k, _):
         pl.semaphore_signal(
-            barrier, inc=1, device_id=(grp, day, flipped(me, k, n)), device_id_type=mesh_id
+            barrier, inc=1, device_id=(grp, day, flipped(me, n - k, n)), device_id_type=mesh_id
         )
         return 0
 

time: 52 us -> 52 us (level)
  no operation moved by 1% of the time
where the time goes in v5:
time: 52 us; the launch traced here: 51.8 us
  Pallas kernels  51.8 us (100%)
    pallas_call x1, Pallas kernels, body(): pl.pallas_call(functools.partial(kernel, n, dates, most, capacity), out_s...  49.7 us
    pallas_call x1, Pallas kernels, body(): pl.pallas_call(functools.partial(place, capacity), out_shape=jax.ShapeDty...  2.1 us

profile of v5, /device:TPU:2, one launch (start us, length us, event | category | flops | bytes accessed | tf_op | source)
XLA Modules:
  0.0 51.8 jit_solution(7499111511786049260)
XLA Ops:
  0.0 49.7 %shard_map.154 = (bf16[17,2,2,128,128]{4,3,2,1,0:T(8,128)(2,1)S(1)}, s32[16]{0:T(128)}) custom-call(s32[1,64]{1,0:T(1,128)} %owner_ref.1, s32[1,64]{1,0:T(1,128)} %slot_ref.1, s32[1,64]{1,0:T(1,128)} %kinds_ref.1, bf16[2,16,8192]{2,1,0:T(8,128)(2,1)} %bitcast.2, f32[2,8192]{1,0:T(2,128)} %rref_hbm.1, bf16[2,128,1024]{2,1,0:T(8,128)(2,1)} %aref_hbm.1, ...), custom_call_target="tpu_custom_call" | custom-call | tf_op jit(solution)/shard_map/pallas_call | solution.py:763
  49.7 2.1 %shard_map.155 = bf16[16,2,2,128,128]{4,3,2,1,0:T(8,128)(2,1)} custom-call(s32[16]{0:T(128)} %get-tuple-element.7.entry_ref, bf16[17,2,2,128,128]{4,3,2,1,0:T(8,128)(2,1)S(1)} %get-tuple-element.8.fil), custom_call_target="tpu_custom_call" | custom-call | tf_op jit(solution)/shard_map/pallas_call | solution.py:809
